TPU v7x, 128 devices: a whole 4x4x4 slice. The times are simulated.
128 devices in a mesh: group: 32 (over z_lo, y, x), cls: 4 (over z_hi, core).
Axes of the slice: x: 4, y: 4, z: 4 (z_hi: 2, z_lo: 2; z = z_hi * 2 + z_lo), core: 2. Of those that a mesh axis runs over, the one named last changes fastest.
Arguments:
- features: bfloat16 [32768, 512], P(('group', 'cls')), may hold values from -6 to 6
- student_logits: bfloat16 [32768, 6656], P('group', 'cls'), may hold values from -100 to 320
- line_lengths: int32 [128], P(('group', 'cls')), may hold values from 64 to 256, as said below
- teacher_group: int32 [1], replicated, may hold values from 0 to 31
- pointwise_weight: bfloat16 [32, 512, 512], P('group'), may hold values from -0.25 to 0.25
- up_weight: bfloat16 [32, 512, 2048], P('group'), may hold values from -0.25 to 0.25
- down_weight: bfloat16 [32, 2048, 512], P('group'), may hold values from -0.125 to 0.125
- class_weight: bfloat16 [32, 512, 6656], P('group', None, 'cls'), may hold values from -9 to 9
- conv_kernel: bfloat16 [32, 3, 512], P('group'), may hold values from -3 to 3
- norm_gains: bfloat16 [32, 2, 512], P('group'), may hold values from 0.5 to 1.5
Outputs:
- divergence: float32 [32768], P(('group', 'cls'))
Inputs may be any that keep to these rules, and one draw needn't show every extreme that they name: `line_lengths`: every line has at least 64 frames in use, and some line uses all 256.
All inputs are finite; a program needn't handle non-finite values.
Results may differ from a plain program's by a relative error of at most 0.035.
Values may be sent and summed in bfloat16 or wider, within the bound.
A program may use at most 64 MiB of HBM per device.

v0:
```python
import math
import jax
import jax.numpy as jnp
from jax import lax
from jax.sharding import PartitionSpec as P

FRAMES = 256
EPS = 1e-06


def spread(x, axis, root):
    mine = lax.axis_index(axis) == root
    return lax.psum(jnp.where(mine, x, jnp.zeros_like(x)), axis)


def frame_mask(line_lengths):
    positions = jnp.arange(FRAMES, dtype=jnp.int32)
    return (positions[None, :] < line_lengths[:, None]).astype(jnp.float32).reshape(-1)


def rms_scale(values, gain):
    return (
        values
        * lax.rsqrt(jnp.mean(values * values, axis=-1, keepdims=True) + EPS)
        * gain.astype(jnp.float32)
    )


def teacher_layer(
    features, line_lengths, pointwise, up_proj, down_proj, kernel, gain_first, gain_second
):
    mask = frame_mask(line_lengths)
    inputs = features.astype(jnp.float32)
    masked = (inputs * mask[:, None]).reshape(-1, FRAMES, inputs.shape[1])
    padded = jnp.pad(masked, ((0, 0), (1, 1), (0, 0)))
    kern = kernel.astype(jnp.float32)
    conv = kern[0] * padded[:, :-2] + kern[1] * padded[:, 1:-1] + kern[2] * padded[:, 2:]
    conv = conv.reshape(inputs.shape).astype(jnp.bfloat16)
    resid = inputs + jnp.dot(conv, pointwise, preferred_element_type=jnp.float32)
    normed = rms_scale(resid, gain_first).astype(jnp.bfloat16)
    hidden = jax.nn.gelu(jnp.dot(normed, up_proj, preferred_element_type=jnp.float32)).astype(
        jnp.bfloat16
    )
    output = resid + jnp.dot(hidden, down_proj, preferred_element_type=jnp.float32)
    return (rms_scale(output, gain_second).astype(jnp.bfloat16), mask)


def row_kl(teacher_rows, student_rows):
    teach = teacher_rows.astype(jnp.float32)
    stud = student_rows.astype(jnp.float32)
    t_max = jnp.max(teach, axis=-1, keepdims=True)
    t_exp = jnp.exp(teach - t_max)
    t_sum = jnp.sum(t_exp, axis=-1)
    s_max = jnp.max(stud, axis=-1, keepdims=True)
    s_sum = jnp.sum(jnp.exp(stud - s_max), axis=-1)
    cross = jnp.sum(t_exp * (teach - stud), axis=-1)
    return cross / t_sum - (t_max[:, 0] + jnp.log(t_sum)) + (s_max[:, 0] + jnp.log(s_sum))


def blocked_rows(row_fn, teacher_logits, student_logits):
    rows = teacher_logits.shape[0]
    block = math.gcd(rows, 512)
    count = rows // block
    pairs = (teacher_logits.reshape(count, block, -1), student_logits.reshape(count, block, -1))
    result = lax.map(lambda pair: row_fn(pair[0], pair[1]), pairs)
    return result.reshape(rows)


def body(
    features,
    student_logits,
    line_lengths,
    teacher_group,
    pointwise_weight,
    up_weight,
    down_weight,
    class_weight,
    conv_kernel,
    norm_gains,
):
    source = teacher_group[0]
    small_params = jnp.concatenate([conv_kernel[0], norm_gains[0]], axis=0)
    pointwise, up_proj, down_proj, params_all, classes = (
        spread(pointwise_weight[0], "group", source),
        spread(up_weight[0], "group", source),
        spread(down_weight[0], "group", source),
        spread(small_params, "group", source),
        spread(class_weight[0], "group", source),
    )
    final, mask = teacher_layer(
        features,
        line_lengths,
        pointwise,
        up_proj,
        down_proj,
        params_all[:3],
        params_all[3],
        params_all[4],
    )
    teacher_logits = jnp.dot(
        lax.all_gather(final, "cls", axis=0, tiled=True),
        classes,
        preferred_element_type=jnp.float32,
    ).astype(jnp.bfloat16)
    teacher_rows, student_rows = (
        lax.all_to_all(teacher_logits, "cls", split_axis=0, concat_axis=1, tiled=True),
        lax.all_to_all(student_logits, "cls", split_axis=0, concat_axis=1, tiled=True),
    )
    divergence = blocked_rows(row_kl, teacher_rows, student_rows)
    return divergence * mask


def solution(mesh):
    return jax.shard_map(
        body,
        mesh=mesh,
        in_specs=(
            P(("group", "cls"), None),
            P("group", "cls"),
            P(("group", "cls")),
            P(),
            P("group", None, None),
            P("group", None, None),
            P("group", None, None),
            P("group", None, "cls"),
            P("group", None, None),
            P("group", None, None),
        ),
        out_specs=P(("group", "cls")),
        check_vma=False,
    )
```

profile of v0, /device:TPU:1, one launch (start us, length us, event | category | flops | bytes accessed | tf_op | source)
XLA Modules:
  0.0 452.9 jit_solution(15250304646624009235)
XLA Ops:
  6.5 0.0 all-reduce.4.cloned.1.call-start
  7.2 0.0 copy-start
  7.2 1.5 select_bitcast_fusion
  8.7 0.9 copy-done
  9.5 1.5 select_bitcast_fusion.1
  11.0 0.7 copy-done.1
  11.8 1.3 select_bitcast_fusion.2
  13.1 0.0 copy-done.2
  13.1 0.8 select_bitcast_fusion.3
  13.9 0.0 all-reduce.4.cloned.1.call-update
  13.9 0.0 copy-start.3
  14.0 0.0 copy-start.4
  14.0 6.6 %all-to-all-start.1 = ((bf16[4,256,1664]{2,1,0:T(8,128)(2,1)}), bf16[4,256,1664]{2,1,0:T(8,128)(2,1)S(1)}, u32[]{:S(2)}, u32[]{:S(2)}) async-start(bf16[4,256,1664]{2,1,0:T(8,128)(2,1)} %bitcast.47), calls=%async_computation.1 | async-start | bytes 6815744 | tf_op jit(solution)/shard_map/all_to_all | solution.py:107
  20.6 0.0 all-gather.2.cloned.1.call-start
  21.3 0.0 copy-done.3
  21.3 0.0 copy-done.4
  21.3 72.6 %psum.35 = bf16[5,512]{1,0:T(8,128)(2,1)S(1)} all-reduce(bf16[5,512]{1,0:T(8,128)(2,1)S(1)} %maximum_select_fusion), channel_id=1, replica_groups=mesh['group'=32,'cls'=4] {'group'}, use_global_device_ids=true, to_apply=%region_0.1 | all-reduce | flops 2560 | bytes 10240 | tf_op jit(solution)/shard_map/psum | solution.py:13
  94.0 1.9 fusion.19
  95.9 237.7 %all-reduce.4.cloned.1.call-done = (bf16[512,512]{1,0:T(8,128)(2,1)}, bf16[2048,512]{1,0:T(8,128)(2,1)}, bf16[512,2048]{1,0:T(8,128)(2,1)}, bf16[512,1664]{1,0:T(8,128)(2,1)}) async-done(((bf16[512,512]{1,0:T(8,128)(2,1)}, bf16[2048,512]{1,0:T(8,128)(2,1)}, bf16[512,2048]{1,0:T(8,128)(2,1)}, bf16[512,1664]{1,0:T(8,128)(2,1)}), (bf16[512,512]{1,0:T(8,128)(2,1)}, bf16[2048,512]{1,0:T(8,128)(2,1)}, ...) | async-done | bytes 6422544 | tf_op jit(solution)/shard_map/psum | solution.py:13
  333.6 2.7 multiply_reduce_fusion.1
  336.3 4.9 %multiply_reduce_fusion = (f32[256]{0:T(256)S(1)}, f32[256,512]{1,0:T(8,128)}) fusion(f32[256,512]{1,0:T(8,128)} %get-tuple-element.30, bf16[2048,512]{1,0:T(8,128)(2,1)} %get-tuple-element.21, bf16[512,2048]{1,0:T(8,128)(2,1)} %get-tuple-element.22, f32[512]{0:T(512)S(1)} %bitcast.51, f32[256]{0:T(256)S(1)} %add_rsqrt_fusion.1), kind=kOutput, calls=%fused_computation.35 | convolution fusion | flops 1079246592 | bytes 5246976 | tf_op jit(solution)/shard_map/dot_general | solution.py:44
  341.2 1.9 multiply_convert_fusion
  343.0 0.0 all-gather.2.cloned.1.call-update
  343.0 43.1 %all-gather.2.cloned.1.call-done = bf16[1024,512]{1,0:T(8,128)(2,1)} async-done(((bf16[256,512]{1,0:T(8,128)(2,1)}), bf16[1024,512]{1,0:T(8,128)(2,1)}) %all-gather.2.cloned.1.call-update) | async-done | bytes 1048592 | tf_op jit(solution)/shard_map/all_gather | solution.py:101
  386.1 5.6 %convolution_convert_fusion = bf16[1024,1664]{1,0:T(8,128)(2,1)} fusion(bf16[1024,512]{1,0:T(8,128)(2,1)} %all-gather.2.cloned.1.call-done, bf16[512,1664]{1,0:T(8,128)(2,1)} %get-tuple-element.23), kind=kOutput, calls=%fused_computation.9 | convolution fusion | flops 1746534400 | bytes 6160384 | tf_op jit(solution)/shard_map/dot_general | solution.py:100
  391.7 0.0 all-to-all-done.1
  391.7 5.0 %all-to-all-start = ((bf16[4,256,1664]{2,1,0:T(8,128)(2,1)}), bf16[4,256,1664]{2,1,0:T(8,128)(2,1)}, u32[]{:S(2)}, u32[]{:S(2)}) async-start(bf16[4,256,1664]{2,1,0:T(8,128)(2,1)} %bitcast.48), calls=%async_computation | async-start | bytes 6815744 | tf_op jit(solution)/shard_map/all_to_all | solution.py:106
  396.6 0.6 reduce_max.32
  397.2 39.8 %all-to-all-done = bf16[4,256,1664]{2,1,0:T(8,128)(2,1)} async-done(((bf16[4,256,1664]{2,1,0:T(8,128)(2,1)}), bf16[4,256,1664]{2,1,0:T(8,128)(2,1)}, u32[]{:S(2)}, u32[]{:S(2)}) %all-to-all-start) | async-done | bytes 3407904 | tf_op jit(solution)/shard_map/all_to_all | solution.py:106
  437.0 2.5 reduce_max.30
  439.5 6.0 %fusion.3 = (f32[256]{0:T(256)S(1)}, f32[256]{0:T(256)S(1)}, f32[256]{0:T(256)S(1)}) fusion(bf16[4,256,1664]{2,1,0:T(8,128)(2,1)} %all-to-all-done, bf16[4,256,1664]{2,1,0:T(8,128)(2,1)S(1)} %all-to-all-done.1, f32[256]{0:T(256)S(1)} %reduce_max.31, f32[256]{0:T(256)S(1)} %reduce_max.33), kind=kLoop, calls=%fused_computation.6 | loop fusion | flops 15334656 | bytes 6820864 | tf_op jit(solution)/shard_map/while/body/eval_jaxpr/reduce_sum | solution.py:56
  445.5 0.6 add_select_fusion
  (11 shorter events, 0.1 us)
Async XLA Ops:
  6.5 327.0 %all-reduce.4.cloned.1.call-start = ((), (), s32[]{:S(2)}) async-start(), calls=%async_computation.3 | async-start | bytes 12845056 | tf_op jit(solution)/shard_map/psum | solution.py:13
  7.2 2.3 copy-start
  9.5 2.2 copy-start.1
  11.8 1.3 copy-start.2
  13.9 7.3 %copy-start.3 = (bf16[1,3,512]{2,1,0:T(4,128)(2,1)S(1)}, bf16[1,3,512]{2,1,0:T(4,128)(2,1)}, u32[]{:S(2)}) copy-start(bf16[1,3,512]{2,1,0:T(4,128)(2,1)} %param.18) | copy-start | bytes 9220
  14.0 7.3 %copy-start.4 = (bf16[1,2,512]{2,1,0:T(2,128)(2,1)S(1)}, bf16[1,2,512]{2,1,0:T(2,128)(2,1)}, u32[]{:S(2)}) copy-start(bf16[1,2,512]{2,1,0:T(2,128)(2,1)} %param.19) | copy-start | bytes 6148
  14.0 377.7 %all-to-all-start.1 = ((bf16[4,256,1664]{2,1,0:T(8,128)(2,1)}), bf16[4,256,1664]{2,1,0:T(8,128)(2,1)S(1)}, u32[]{:S(2)}, u32[]{:S(2)}) async-start(bf16[4,256,1664]{2,1,0:T(8,128)(2,1)} %bitcast.47), calls=%async_computation.1 | async-start | bytes 6815744 | tf_op jit(solution)/shard_map/all_to_all | solution.py:107
  20.6 365.5 %all-gather.2.cloned.1.call-start = ((), (), s32[]{:S(2)}) async-start(), calls=%async_computation.2 | async-start | bytes 1310720 | tf_op jit(solution)/shard_map/all_gather | solution.py:101
  391.7 45.3 %all-to-all-start = ((bf16[4,256,1664]{2,1,0:T(8,128)(2,1)}), bf16[4,256,1664]{2,1,0:T(8,128)(2,1)}, u32[]{:S(2)}, u32[]{:S(2)}) async-start(bf16[4,256,1664]{2,1,0:T(8,128)(2,1)} %bitcast.48), calls=%async_computation | async-start | bytes 6815744 | tf_op jit(solution)/shard_map/all_to_all | solution.py:106
Sparse Core Ops, SparseCore 0:
  14.1 319.4 all-reduce.3
  343.2 42.8 all-gather.1
where the time goes:
time: 454 us; the launch traced here: 453 us
  waiting for transfers between devices  321 us (71%)
  blocking collectives  72.6 us (16%)
  other arithmetic  18.6 us (4%)
  between operations  14.8 us (3%)
  matrix products  13.2 us (3%)
  starting transfers between devices  11.6 us (3%)
    psum x1, waiting for transfers between devices, spread(): return lax.psum(jnp.where(mine, x, jnp.zeros_like(x)), axis)  238 us
    psum x1, blocking collectives, spread(): return lax.psum(jnp.where(mine, x, jnp.zeros_like(x)), axis)  72.6 us
    all_gather x1, waiting for transfers between devices, body(): lax.all_gather(final, 'cls', axis=0, tiled=True)  43.1 us
    all_to_all x1, waiting for transfers between devices, body(): lax.all_to_all(teacher_logits, 'cls', split_axis=0, concat_axis=1, tiled=...  39.8 us
  transfers between devices with their start and end apart: 4, of which 3 were waited for; matrix products, arithmetic and copies ran while one was open for 4% of the time, Pallas kernels for 0%

commit v1 on v0

--- a/solution.py
+++ b/solution.py
@@ -6,6 +6,12 @@
 
 FRAMES = 256
 EPS = 1e-06
+
+
+def _cover_copies(u_in):
+    return jnp.concatenate(
+        lax.all_to_all(jnp.stack(lax.axis_size("cls") * [u_in]), "cls", 0, 0), axis=0
+    )
 
 
 def spread(x, axis, root):
@@ -98,9 +104,7 @@
         params_all[4],
     )
     teacher_logits = jnp.dot(
-        lax.all_gather(final, "cls", axis=0, tiled=True),
-        classes,
-        preferred_element_type=jnp.float32,
+        _cover_copies(final), classes, preferred_element_type=jnp.float32
     ).astype(jnp.bfloat16)
     teacher_rows, student_rows = (
         lax.all_to_all(teacher_logits, "cls", split_axis=0, concat_axis=1, tiled=True),

time: 454 us -> 486 us (1.070)
  blocking collectives: 72.6 us -> 113 us
    all_gather x1 -> x0, waiting for transfers between devices: 43.1 us -> none  [body(): lax.all_gather(final, 'cls', axis=0, tiled=True)]
    all_to_all x0 -> x1, blocking collectives: none -> 40.2 us  [_cover_copies(): lax.all_to_all(jnp.stack(lax.axis_size('cls') * [u_in]), 'cls', 0, 0)]
    all_to_all x1, waiting for transfers between devices: 0.01 us -> 34.7 us  [body(): lax.all_to_all(student_logits, 'cls', split_axis=0, concat_axis=1, tiled=...]
    psum x1, waiting for transfers between devices: 238 us -> 245 us  [spread(): return lax.psum(jnp.where(mine, x, jnp.zeros_like(x)), axis)]
  transfers between devices with their start and end apart: 4 -> 3, of which waited for: 3 -> 3; matrix products, arithmetic and copies ran while one was open for 4% -> 1% of each run, Pallas kernels for 0% -> 0%
where the time goes in v1:
time: 486 us
  waiting for transfers between devices  320 us (66%)
  blocking collectives  113 us (23%)
  other arithmetic  15.1 us (3%)
  between operations  14.9 us (3%)
  matrix products  10.5 us (2%)
  starting transfers between devices  10.4 us (2%)
    psum x1, waiting for transfers between devices, spread(): return lax.psum(jnp.where(mine, x, jnp.zeros_like(x)), axis)  245 us
    psum x1, blocking collectives, spread(): return lax.psum(jnp.where(mine, x, jnp.zeros_like(x)), axis)  72.9 us
    all_to_all x1, blocking collectives, _cover_copies(): lax.all_to_all(jnp.stack(lax.axis_size('cls') * [u_in]), 'cls', 0, 0)  40.2 us
    all_to_all x1, waiting for transfers between devices, body(): lax.all_to_all(teacher_logits, 'cls', split_axis=0, concat_axis=1, tiled=...  39.8 us
    all_to_all x1, waiting for transfers between devices, body(): lax.all_to_all(student_logits, 'cls', split_axis=0, concat_axis=1, tiled=...  34.7 us
  transfers between devices with their start and end apart: 3, of which 3 were waited for; matrix products, arithmetic and copies ran while one was open for 1% of the time, Pallas kernels for 0%

profile of v1, /device:TPU:1, one launch (start us, length us, event | category | flops | bytes accessed | tf_op | source)
XLA Modules:
  0.0 485.6 jit_solution(11557771372432222627)
XLA Ops:
  6.5 0.0 all-reduce.4.cloned.1.call-start
  7.2 0.0 copy-start
  7.2 1.5 select_bitcast_fusion
  8.7 0.9 copy-done
  9.5 0.0 copy-start.1
  9.5 1.5 select_bitcast_fusion.1
  11.0 0.7 copy-done.1
  11.8 1.3 select_bitcast_fusion.2
  13.1 0.0 copy-done.2
  13.1 0.8 select_bitcast_fusion.3
  13.9 0.0 all-reduce.4.cloned.1.call-update
  14.6 0.0 copy-done.4
  14.7 0.0 copy-done.5
  14.7 72.9 %psum.35 = bf16[5,512]{1,0:T(8,128)(2,1)S(1)} all-reduce(bf16[5,512]{1,0:T(8,128)(2,1)S(1)} %maximum_select_fusion), channel_id=1, replica_groups=mesh['group'=32,'cls'=4] {'group'}, use_global_device_ids=true, to_apply=%region_0.1 | all-reduce | flops 2560 | bytes 10240 | tf_op jit(solution)/shard_map/psum | solution.py:19
  87.6 0.0 copy-done.3
  87.7 0.1 fusion.19
  87.8 245.4 %all-reduce.4.cloned.1.call-done = (bf16[512,512]{1,0:T(8,128)(2,1)}, bf16[2048,512]{1,0:T(8,128)(2,1)}, bf16[512,2048]{1,0:T(8,128)(2,1)}, bf16[512,1664]{1,0:T(8,128)(2,1)}) async-done(((bf16[512,512]{1,0:T(8,128)(2,1)}, bf16[2048,512]{1,0:T(8,128)(2,1)}, bf16[512,2048]{1,0:T(8,128)(2,1)}, bf16[512,1664]{1,0:T(8,128)(2,1)}), (bf16[512,512]{1,0:T(8,128)(2,1)}, bf16[2048,512]{1,0:T(8,128)(2,1)}, ...) | async-done | bytes 6422544 | tf_op jit(solution)/shard_map/psum | solution.py:19
  333.2 1.7 multiply_reduce_fusion.1
  334.9 0.1 copy-done.6
  334.9 3.3 multiply_reduce_fusion
  338.2 0.1 multiply_convert_fusion
  338.3 0.1 stack.2
  338.4 40.2 %all_to_all.31 = bf16[4,256,512]{2,1,0:T(8,128)(2,1)} all-to-all(bf16[4,256,512]{2,1,0:T(8,128)(2,1)S(1)} %stack.2), channel_id=1, replica_groups=mesh['group'=32,'cls'=4] {'cls'}, dimensions={0} | all-to-all | bytes 2097152 | tf_op jit(solution)/shard_map/all_to_all | solution.py:13
  378.6 4.7 all-to-all-start.2
  383.4 5.6 %convolution_convert_fusion = bf16[1024,1664]{1,0:T(8,128)(2,1)} fusion(bf16[1024,512]{1,0:T(8,128)(2,1)} %bitcast.50, bf16[512,1664]{1,0:T(8,128)(2,1)} %get-tuple-element.23), kind=kOutput, calls=%fused_computation.9 | convolution fusion | flops 1746534400 | bytes 6160384 | tf_op jit(solution)/shard_map/dot_general | solution.py:106
  388.9 34.7 %all-to-all-done.2 = bf16[4,256,1664]{2,1,0:T(8,128)(2,1)S(1)} async-done(((bf16[4,256,1664]{2,1,0:T(8,128)(2,1)}), bf16[4,256,1664]{2,1,0:T(8,128)(2,1)S(1)}, u32[]{:S(2)}, u32[]{:S(2)}) %all-to-all-start.2) | async-done | bytes 3407904 | tf_op jit(solution)/shard_map/all_to_all | solution.py:111
  423.6 5.6 %all-to-all-start.1 = ((bf16[4,256,1664]{2,1,0:T(8,128)(2,1)}), bf16[4,256,1664]{2,1,0:T(8,128)(2,1)}, u32[]{:S(2)}, u32[]{:S(2)}) async-start(bf16[4,256,1664]{2,1,0:T(8,128)(2,1)} %bitcast.49), calls=%async_computation.1 | async-start | bytes 6815744 | tf_op jit(solution)/shard_map/all_to_all | solution.py:110
  429.2 0.6 reduce_max.32
  429.8 39.8 %all-to-all-done.1 = bf16[4,256,1664]{2,1,0:T(8,128)(2,1)} async-done(((bf16[4,256,1664]{2,1,0:T(8,128)(2,1)}), bf16[4,256,1664]{2,1,0:T(8,128)(2,1)}, u32[]{:S(2)}, u32[]{:S(2)}) %all-to-all-start.1) | async-done | bytes 3407904 | tf_op jit(solution)/shard_map/all_to_all | solution.py:110
  469.6 2.5 reduce_max.30
  472.1 6.0 %fusion.3 = (f32[256]{0:T(256)S(1)}, f32[256]{0:T(256)S(1)}, f32[256]{0:T(256)S(1)}) fusion(bf16[4,256,1664]{2,1,0:T(8,128)(2,1)} %all-to-all-done.1, bf16[4,256,1664]{2,1,0:T(8,128)(2,1)S(1)} %all-to-all-done.2, f32[256]{0:T(256)S(1)} %reduce_max.31, f32[256]{0:T(256)S(1)} %reduce_max.33), kind=kLoop, calls=%fused_computation.6 | loop fusion | flops 15334656 | bytes 6820864 | tf_op jit(solution)/shard_map/while/body/eval_jaxpr/reduce_sum | solution.py:62
  478.1 0.6 add_select_fusion
  (14 shorter events, 0.1 us)
Async XLA Ops:
  6.5 326.6 %all-reduce.4.cloned.1.call-start = ((), (), s32[]{:S(2)}) async-start(), calls=%async_computation.3 | async-start | bytes 12845056 | tf_op jit(solution)/shard_map/psum | solution.py:19
  7.2 2.3 copy-start
  9.5 2.2 copy-start.1
  11.8 1.3 copy-start.2
  13.9 0.7 copy-start.4
  13.9 0.7 copy-start.5
  13.9 73.7 %copy-start.3 = (bf16[256,512]{1,0:T(8,128)(2,1)S(1)}, bf16[256,512]{1,0:T(8,128)(2,1)}, u32[]{:S(2)}) copy-start(bf16[256,512]{1,0:T(8,128)(2,1)} %param.10) | copy-start | bytes 786436
  333.2 1.7 copy-start.6
  378.6 45.0 %all-to-all-start.2 = ((bf16[4,256,1664]{2,1,0:T(8,128)(2,1)}), bf16[4,256,1664]{2,1,0:T(8,128)(2,1)S(1)}, u32[]{:S(2)}, u32[]{:S(2)}) async-start(bf16[4,256,1664]{2,1,0:T(8,128)(2,1)} %bitcast.48), calls=%async_computation.2 | async-start | bytes 6815744 | tf_op jit(solution)/shard_map/all_to_all | solution.py:111
  423.6 46.0 %all-to-all-start.1 = ((bf16[4,256,1664]{2,1,0:T(8,128)(2,1)}), bf16[4,256,1664]{2,1,0:T(8,128)(2,1)}, u32[]{:S(2)}, u32[]{:S(2)}) async-start(bf16[4,256,1664]{2,1,0:T(8,128)(2,1)} %bitcast.49), calls=%async_computation.1 | async-start | bytes 6815744 | tf_op jit(solution)/shard_map/all_to_all | solution.py:110
Sparse Core Ops, SparseCore 0:
  14.1 319.0 all-reduce.3
